TPU v7x, 32 devices: a whole 2x2x4 slice. The times are simulated.
32 devices in a mesh: tm: 8 (over z, x), lon: 4 (over y, core).
Axes of the slice: x: 2, y: 2, z: 4, core: 2. Of those that a mesh axis runs over, the one named last changes fastest.
Arguments:
- start: float32 [3, 128, 512], P(None, 'lon'), may hold values from -6 to 6
- depth: float32 [128, 512], P('lon'), may hold values from 0.5 to 1.5
Outputs:
- ends: float32 [8, 3, 128, 512], P('tm', None, 'lon')
All inputs are finite; a program needn't handle non-finite values.
Results may differ from a plain program's by a relative error of at most 0.00002.
Values sent between devices are 32-bit elements; how exact they have to be, the bound alone decides.
No kernel may reach another device: no remote copies, remote signals or barrier semaphores. Data moves between devices by JAX's collectives and lax.ppermute only.
A program may use at most 64 MiB of HBM per device.

v0:
```python
import math

import jax
import jax.numpy as jnp
import numpy as np
from jax import lax
from jax.experimental import pallas as pl
from jax.experimental.pallas import tpu as pltpu
from jax.sharding import PartitionSpec as P

STEPS = 3
ROUNDS = 2
LAT_LIMIT = 1.2
COURANT = 1.2
DEPTH_MAX = 1.5
GRAVITY = 1.0
TURN_RATE = 0.15

HALO = 2 * STEPS * ROUNDS
ROWS = 8
LANES = 128
DEAL_ROWS = 64
FIRST, MORE = 3, 4
VMEM_LIMIT = 24 << 20

EAST, POLE, DIVERGE, SPIN_U, SPIN_V, GRAD_E, GRAD_N, TURN_C, TURN_U, TURN_V, EAST_INV, POLE_INV = range(12)


def lat_table(lon_cells, lat_cells):
    latitude = -LAT_LIMIT + (np.arange(lat_cells) + 0.5) * (2.0 * LAT_LIMIT / lat_cells)
    cosine = np.cos(latitude)
    north_spacing = 2.0 * LAT_LIMIT / lat_cells
    east_spacing = cosine * (2.0 * math.pi / lon_cells)
    narrowest = math.cos(LAT_LIMIT - LAT_LIMIT / lat_cells) * 2.0 * math.pi / lon_cells
    time_step = COURANT / (
        math.sqrt(DEPTH_MAX * GRAVITY) * math.sqrt(1.0 / narrowest**2 + 1.0 / north_spacing**2)
    )
    spin = TURN_RATE * np.sin(latitude)
    turning = spin * STEPS
    east = time_step / (2.0 * east_spacing)
    north = time_step / (2.0 * north_spacing)
    rows = [None] * 12
    rows[EAST] = east
    rows[POLE] = cosine
    rows[DIVERGE] = north / cosine
    rows[SPIN_U] = spin * east / cosine
    rows[SPIN_V] = spin * cosine / east
    rows[GRAD_E] = GRAVITY * east
    rows[GRAD_N] = GRAVITY * north + 0.0 * cosine
    rows[TURN_C] = np.cos(turning)
    rows[TURN_U] = np.sin(turning) * east / cosine
    rows[TURN_V] = np.sin(turning) * cosine / east
    rows[EAST_INV] = 1.0 / east
    rows[POLE_INV] = 1.0 / cosine
    table = np.stack(rows).astype(np.float32)
    return table.reshape(12, LANES, lat_cells // LANES).swapaxes(1, 2).reshape(12, lat_cells)


def windows(low, high):
    starts = list(range(low, high - ROWS + 1, ROWS))
    if starts[-1] + ROWS < high:
        starts.append(high - ROWS)
    return starts


def deal(tiles, dealing, undealing):
    def block(index, carry):
        start = pl.multiple_of(index * DEAL_ROWS, DEAL_ROWS)
        row = start + lax.broadcasted_iota(jnp.int32, (DEAL_ROWS, LANES), 0)
        lane = lax.broadcasted_iota(jnp.int32, (DEAL_ROWS, LANES), 1)
        place = row % LANES * tiles + row // LANES
        for t in range(tiles):
            hit = row == lane * tiles + t
            dealing[pl.ds(start, DEAL_ROWS), lanes(t)] = jnp.where(hit, 1.0, 0.0).astype(jnp.bfloat16)
            hit = place == lane + t * LANES
            undealing[pl.ds(start, DEAL_ROWS), lanes(t)] = jnp.where(hit, 1.0, 0.0).astype(jnp.bfloat16)
        return carry

    lax.fori_loop(0, tiles * LANES // DEAL_ROWS, block, 0)


def times_one_hot(values, matrix):
    pieces = []
    rest = values
    for _ in range(3):
        pieces.append(rest.astype(jnp.bfloat16))
        rest = rest - pieces[-1].astype(jnp.float32)
    count = values.shape[0]
    out = jnp.dot(jnp.concatenate(pieces, axis=0), matrix, preferred_element_type=jnp.float32)
    return out[:count] + out[count : 2 * count] + out[2 * count :]


def lanes(t):
    return slice(t * LANES, (t + 1) * LANES)


def put_fields(dealt, table, tiles, count, first_row, step, refs, base):
    for t in range(tiles):
        h, u, v, d = (
            dealt[first_row + f * step : first_row + f * step + count, lanes(t)] for f in range(4)
        )
        he = d * table[EAST, :1, lanes(t)]
        hp = d * table[POLE, :1, lanes(t)]
        rows = slice(base, base + count)
        values = (h, u * he, v * hp, he * table[GRAD_E, :1, lanes(t)], hp * table[GRAD_N, :1, lanes(t)])
        for ref, value in zip(refs, values):
            ref[t, rows, :] = value


def windows(low, high):
    starts = list(range(low, high - ROWS + 1, ROWS))
    if starts[-1] + ROWS < high:
        starts.append(high - ROWS)
    return starts


def shrinking(low, high):
    return [
        (windows(low + 2 * s - 1, high - 2 * s + 1), windows(low + 2 * s, high - 2 * s))
        for s in range(1, STEPS + 1)
    ]


def strips(wide):
    offsets = range(0, HALO, ROWS)
    return [
        (
            [2 * s - 1 + k for k in offsets] + [wide - 2 * s + 1 - ROWS - k for k in offsets],
            [2 * s + k for k in offsets] + [wide - 2 * s - ROWS - k for k in offsets],
        )
        for s in range(1, STEPS + 1)
    ]


def joints(low, high):
    return [(low + 2 * s + 3, high - 2 * s - 3 - ROWS) for s in range(1, STEPS)]


def at(ref, t, row):
    return ref[t, row : row + ROWS, :]


def put(ref, t, row, value):
    ref[t, row : row + ROWS, :] = value


class Fluid:
    def __init__(self, table, tiles, grad_e, grad_n):
        lane = lax.broadcasted_iota(jnp.int32, (ROWS, LANES), 1)
        self.first, self.last = lane == 0, lane == LANES - 1
        self.table, self.tiles = table, tiles
        self.grad_e, self.grad_n = grad_e, grad_n

    def const(self, row, t):
        return self.table[row, :, lanes(t)]

    def consts(self, *rows):
        return [[self.const(row, t) for t in range(self.tiles)] for row in rows]

    def north_diff(self, parts):
        wrapped = pltpu.roll(parts[0], LANES - 1, 1)
        above = parts[1:] + [jnp.where(self.last, 0.0, wrapped)]
        wrapped = pltpu.roll(parts[-1], 1, 1)
        below = [jnp.where(self.first, 0.0, wrapped)] + parts[:-1]
        return [up - down for up, down in zip(above, below)]

    def turn(self, a, b, t):
        c = self.const(TURN_C, t)
        return c * a + self.const(TURN_U, t) * b, c * b - self.const(TURN_V, t) * a

    def fine(self, state, temps, plan, finish):
        tiles = range(self.tiles)
        for step, (height_rows, rest_rows) in enumerate(plan):
            height, alpha, beta = state
            new_h, new_a, new_b = temps[step]
            (diverge,) = self.consts(DIVERGE)
            for row in height_rows:
                flux = self.north_diff([at(beta, t, row) for t in tiles])
                for t in tiles:
                    value = at(height, t, row) - (at(alpha, t, row + 1) - at(alpha, t, row - 1))
                    put(new_h, t, row, value - diverge[t] * flux[t])
            spin_u, spin_v = self.consts(SPIN_U, SPIN_V)
            for row in rest_rows:
                here = [at(new_h, t, row) for t in tiles]
                slope = self.north_diff(here)
                for t in tiles:
                    b = at(beta, t, row)
                    east = at(new_h, t, row + 1) - at(new_h, t, row - 1)
                    a = at(alpha, t, row) + spin_u[t] * b - at(self.grad_e, t, row) * east
                    b = b - spin_v[t] * a - at(self.grad_n, t, row) * slope[t]
                    if step == STEPS - 1:
                        finish(t, row, here[t], a, b)
                    else:
                        put(new_a, t, row, a)
                        put(new_b, t, row, b)
            state = (new_h, new_a, new_b)

    def turn_rows(self, source, target, rows):
        for row in rows:
            for t in range(self.tiles):
                a, b = self.turn(at(source[0], t, row), at(source[1], t, row), t)
                put(target[0], t, row, a)
                put(target[1], t, row, b)


def stages(refs):
    return [refs[0:3], refs[3:6], (refs[6], None, None)]


def streams_of(refs):
    return [stages(refs[7 * k : 7 * k + 7]) for k in range(len(refs) // 7)]


def in_blocks(number, one_block):
    one_block(0, FIRST)

    def more(index, carry):
        one_block(FIRST + MORE * index, MORE)
        return carry

    lax.fori_loop(0, (number + MORE - FIRST - 1) // MORE, more, 0)


def prepare(cells, tiles, stacked, out, table, dealing, undealing, inner, joint, *scratch):
    number = lax.axis_index("tm")
    for row in range(table.shape[0]):
        source = stacked[4 * cells + row : 4 * cells + row + 1, :]
        table[row] = jnp.broadcast_to(source, (ROWS, tiles * LANES))
    deal(tiles, dealing, undealing)
    dealt = times_one_hot(stacked[: 4 * cells, :], dealing[...])
    put_fields(dealt, table, tiles, cells, 0, cells, [out.at[k] for k in range(5)], 0)
    for t in range(tiles):
        over = 1.0 / dealt[3 * cells :, lanes(t)]
        out[5, t] = over * table[EAST_INV, :1, lanes(t)]
        out[6, t] = over * table[POLE_INV, :1, lanes(t)]

    fluid = Fluid(table, tiles, out.at[3], out.at[4])
    reach = 2 * STEPS
    plan = shrinking(0, cells)
    guesses = [scratch[2 * k : 2 * k + 2] for k in range(MORE)]
    temps_of = streams_of(scratch[2 * MORE :])
    guesses[0][0][...] = out[1]
    guesses[0][1][...] = out[2]
    for field in range(3):
        inner[0, field, :, : cells - 2 * reach, :] = out[field, :, reach : cells - reach, :]
    every = range(0, cells, ROWS)

    def one_block(start, count):
        for k in range(count):
            one_slice(start + k, guesses[k], temps_of[k])
            fluid.turn_rows(guesses[k], guesses[(k + 1) % count], every)

    def one_slice(m, guess, temps):
        before = [inner.at[m, field] for field in range(3)]
        after = [inner.at[m + 1, field] for field in range(3)]

        def finish(t, row, h, a, b):
            own_row = row - reach
            put(after[0], t, own_row, h + (at(before[0], t, own_row) - out[0, t, row : row + ROWS, :]))
            da, db = fluid.turn(
                at(before[1], t, own_row) - at(guess[0], t, row),
                at(before[2], t, own_row) - at(guess[1], t, row),
                t,
            )
            put(after[1], t, own_row, a + da)
            put(after[2], t, own_row, b + db)

        fluid.fine((out.at[0], *guess), temps, plan, finish)
        for step, sides in enumerate(joints(0, cells)):
            for side, row in enumerate(sides):
                for field in range(3):
                    for t in range(tiles):
                        joint[m, step, side, field, t] = at(temps[step][field], t, row)

    in_blocks(number, one_block)


def kernel(cells, tiles, own, left, right, table, dealing, undealing, inner, joint, ends, *scratch):
    (s_h, grad_e, grad_n, w_h, w_a, w_b, firsts, flat) = scratch[:8]
    guesses = [scratch[8 + 2 * k : 10 + 2 * k] for k in range(MORE)]
    temps_of = streams_of(scratch[8 + 2 * MORE :])
    wide = cells + 2 * HALO
    reach = 2 * STEPS
    number = lax.axis_index("tm")
    fluid = Fluid(table, tiles, grad_e, grad_n)

    fields = (s_h, *guesses[0], grad_e, grad_n)
    for side, halo in enumerate((left, right)):
        for field in range(4):
            first_row = (4 * side + field) * HALO
            flat[first_row : first_row + HALO, :] = halo[field]
    dealt = times_one_hot(flat[...], dealing[...])
    put_fields(dealt, table, tiles, HALO, 0, HALO, fields, 0)
    put_fields(dealt, table, tiles, HALO, 4 * HALO, HALO, fields, HALO + cells)
    for k, ref in enumerate(fields):
        ref[:, HALO : HALO + cells, :] = own[k]
    for field, ref in enumerate(fields[:3]):
        firsts[0, field] = ref[...]

    edge_rows = [*range(0, HALO + ROWS, ROWS)]
    edge_rows = sorted({*edge_rows, *(wide - ROWS - row for row in edge_rows)})

    def round_one(m, guess, temps):
        before = [firsts.at[m, field] for field in range(3)]
        after = [firsts.at[m + 1, field] for field in range(3)]

        def finish(t, row, h, a, b):
            put(after[0], t, row, h + (at(before[0], t, row) - at(s_h, t, row)))
            da, db = fluid.turn(
                at(before[1], t, row) - at(guess[0], t, row),
                at(before[2], t, row) - at(guess[1], t, row),
                t,
            )
            put(after[1], t, row, a + da)
            put(after[2], t, row, b + db)

        for step, sides in enumerate(joints(HALO, HALO + cells)):
            for side, row in enumerate(sides):
                for field in range(3):
                    for t in range(tiles):
                        put(temps[step][field], t, row, joint[m, step, side, field, t])
        fluid.fine((s_h, *guess), temps, strips(wide), finish)
        for row in windows(0, cells - 2 * reach):
            for field in range(3):
                for t in range(tiles):
                    put(after[field], t, HALO + reach + row, at(inner.at[m + 1, field], t, row))

    def block_one(start, count):
        for k in range(count):
            round_one(start + k, guesses[k], temps_of[k])
            fluid.turn_rows(guesses[k], guesses[(k + 1) % count], edge_rows)

    def round_two(m, temps):
        first = [firsts.at[m, field] for field in range(3)]
        active = m <= number

        def finish(t, row, h, a, b):
            wh, wa, wb = (at(ref, t, row) for ref in (w_h, w_a, w_b))
            da, db = fluid.turn(wa - at(first[1], t, row), wb - at(first[2], t, row), t)
            put(w_h, t, row, jnp.where(active, h + (wh - at(first[0], t, row)), wh))
            put(w_a, t, row, jnp.where(active, a + da, wa))
            put(w_b, t, row, jnp.where(active, b + db, wb))

        fluid.fine(first, temps, shrinking(reach, wide - reach), finish)

    def block_two(start, count):
        for k in range(count):
            round_two(1 + start + k, temps_of[k])

    in_blocks(number, block_one)
    for field, ref in enumerate((w_h, w_a, w_b)):
        ref[...] = firsts[1, field]

    @pl.when(number > 0)
    def _():
        in_blocks(number, block_two)

    rows = slice(HALO, HALO + cells)
    whole = [
        jnp.concatenate([w_h[t, rows, :] for t in range(tiles)], axis=1),
        jnp.concatenate([w_a[t, rows, :] * own[5, t] for t in range(tiles)], axis=1),
        jnp.concatenate([w_b[t, rows, :] * own[6, t] for t in range(tiles)], axis=1),
    ]
    whole = times_one_hot(jnp.concatenate(whole, axis=0), undealing[...])
    for field in range(3):
        ends[0, field] = whole[field * cells : (field + 1) * cells]


def body(start, depth):
    count = lax.axis_size("lon")
    _, cells, lat_cells = start.shape
    tiles = lat_cells // LANES
    slots = FIRST + MORE * (max(lax.axis_size("tm") - 1 - FIRST + MORE - 1, 0) // MORE)
    table = jnp.asarray(lat_table(cells * count, lat_cells))
    both = jnp.concatenate([start, depth[None]], axis=0)
    ring = [(i, (i + 1) % count) for i in range(count)]
    left = lax.ppermute(both[:, cells - HALO :], "lon", ring)
    right = lax.ppermute(both[:, :HALO], "lon", [(j, i) for i, j in ring])
    stacked = jnp.concatenate([start.reshape(-1, lat_cells), depth, table], axis=0)
    wide = cells + 2 * HALO
    inside = -(-(cells - 4 * STEPS) // ROWS) * ROWS
    vmem = pl.BlockSpec(memory_space=pltpu.VMEM)

    def shape(*dims, dtype=jnp.float32):
        return jax.ShapeDtypeStruct(dims, dtype)

    def scratch(*dims):
        return pltpu.VMEM(dims, jnp.float32)

    params = pltpu.CompilerParams(
        vmem_limit_bytes=VMEM_LIMIT
    )
    prepared = pl.pallas_call(
        lambda *refs: prepare(cells, tiles, *refs),
        out_shape=(
            shape(7, tiles, cells, LANES),
            shape(table.shape[0], ROWS, lat_cells),
            shape(lat_cells, lat_cells, dtype=jnp.bfloat16),
            shape(lat_cells, lat_cells, dtype=jnp.bfloat16),
            shape(slots + 1, 3, tiles, inside, LANES),
            shape(slots, STEPS - 1, 2, 3, tiles, ROWS, LANES),
        ),
        in_specs=[vmem],
        out_specs=[vmem] * 6,
        scratch_shapes=[scratch(tiles, cells, LANES)] * (9 * MORE),
        compiler_params=params,
        cost_estimate=pl.CostEstimate(flops=10**9, bytes_accessed=10**7, transcendentals=0),
        name="prepare",
    )(stacked)
    return pl.pallas_call(
        lambda *refs: kernel(cells, tiles, *refs),
        out_shape=shape(1, *start.shape),
        in_specs=[vmem] * 8,
        out_specs=vmem,
        scratch_shapes=[scratch(tiles, wide, LANES)] * 6
        + [scratch(slots + 1, 3, tiles, wide, LANES), scratch(8 * HALO, lat_cells)]
        + [scratch(tiles, wide, LANES)] * (9 * MORE),
        compiler_params=params,
        name="parareal",
    )(prepared[0], left, right, *prepared[1:])


def solution(mesh):
    return jax.shard_map(
        body,
        mesh=mesh,
        in_specs=(P(None, "lon", None), P("lon", None)),
        out_specs=P("tm", None, "lon", None),
        check_vma=False,
    )
```

profile of v0, /device:TPU:27, one launch (start us, length us, event | category | flops | bytes accessed | tf_op | source)
XLA Modules:
  0.0 11.8 jit_solution(16171088023071836094)
XLA Ops:
  0.0 1.0 %pad_maximum_fusion.1 = (f32[4,12,512]{2,1,0:T(8,128)S(1)}, f32[4,12,512]{2,1,0:T(8,128)S(1)}) fusion(f32[1,32,512]{2,1,0:T(8,128)} %bitcast.3, f32[3,32,512]{2,1,0:T(8,128)} %param.3), kind=kLoop, calls=%fused_computation.4 | loop fusion | flops 49152 | bytes 458752 | tf_op jit(solution)/shard_map/concatenate | solution.py:375
  1.0 1.9 %collective-permute-start = (f32[4,12,512]{2,1,0:T(8,128)S(1)}, f32[4,12,512]{2,1,0:T(8,128)S(1)}, u32[]{:S(2)}, u32[]{:S(2)}) collective-permute-start(f32[4,12,512]{2,1,0:T(8,128)S(1)} %get-tuple-element.18), channel_id=1, source_target_pairs={{0,1},{1,2},{2,3},{3,0},{4,5},{5,6},{6,7},{7,4},{8,9},{9,10},{10,1... | collective-permute-start | bytes 294920 | tf_op jit(solution)/shard_map/ppermute | solution.py:377
  2.9 0.0 collective-permute-start.1
  2.9 1.0 %pad_maximum_fusion.refs_0_ = f32[140,512]{1,0:T(8,128)S(1)} fusion(f32[12,512]{1,0:T(8,128)} %constant.2.clone, f32[32,512]{1,0:T(8,128)} %param.4, f32[96,512]{1,0:T(8,128)} %bitcast.2), kind=kLoop, calls=%fused_computation | loop fusion | flops 143360 | bytes 573440 | tf_op jit(solution)/shard_map/concatenate | solution.py:379
  3.9 2.5 %prepare.1 = (f32[7,4,32,128]{3,2,1,0:T(8,128)S(1)}, f32[12,8,512]{2,1,0:T(8,128)S(1)}, bf16[512,512]{1,0:T(8,128)(2,1)S(1)}, bf16[512,512]{1,0:T(8,128)(2,1)S(1...) custom-call(f32[140,512]{1,0:T(8,128)S(1)} %pad_maximum_fusion.refs_0_), custom_call_target="tpu_custom_call" | custom-call | flops 1000000000 | bytes 10000000 | tf_op jit(solution)/shard_map/prepare/pallas_call | solution.py:393
  6.4 0.0 collective-permute-done.refs_1_
  6.4 0.9 %collective-permute-done.1.refs_2_ = f32[4,12,512]{2,1,0:T(8,128)S(1)} collective-permute-done((f32[4,12,512]{2,1,0:T(8,128)S(1)}, f32[4,12,512]{2,1,0:T(8,128)S(1)}, u32[]{:S(2)}, u32[]{:S(2)}) %collective-permute-start.1) | collective-permute-done | bytes 98336 | tf_op jit(solution)/shard_map/ppermute | solution.py:378
  7.3 4.5 %parareal.1 = f32[1,3,32,512]{3,2,1,0:T(8,128)} custom-call(f32[7,4,32,128]{3,2,1,0:T(8,128)S(1)} %get-tuple-element.11.refs_0_, f32[4,12,512]{2,1,0:T(8,128)S(1)} %collective-permute-done.refs_1_, f32[4,12,512]{2,1,0:T(8,128)S(1)} %collective-permute-done.1.refs_2_, f32[12,8,512]{2,1,0:T(8,128)S(1)} %get-tuple-element.12.refs_3_, ...), custom_call_target="tpu_custom_call" | custom-call | tf_op jit(solution)/shard_map/parareal/pallas_call | solution.py:410
Async XLA Ops:
  1.0 5.4 %collective-permute-start = (f32[4,12,512]{2,1,0:T(8,128)S(1)}, f32[4,12,512]{2,1,0:T(8,128)S(1)}, u32[]{:S(2)}, u32[]{:S(2)}) collective-permute-start(f32[4,12,512]{2,1,0:T(8,128)S(1)} %get-tuple-element.18), channel_id=1, source_target_pairs={{0,1},{1,2},{2,3},{3,0},{4,5},{5,6},{6,7},{7,4},{8,9},{9,10},{10,1... | collective-permute-start | bytes 294920 | tf_op jit(solution)/shard_map/ppermute | solution.py:377
  2.9 4.4 %collective-permute-start.1 = (f32[4,12,512]{2,1,0:T(8,128)S(1)}, f32[4,12,512]{2,1,0:T(8,128)S(1)}, u32[]{:S(2)}, u32[]{:S(2)}) collective-permute-start(f32[4,12,512]{2,1,0:T(8,128)S(1)} %get-tuple-element.17), channel_id=1, source_target_pairs={{1,0},{2,1},{3,2},{0,3},{5,4},{6,5},{7,6},{4,7},{9,8},{10,9},{11,1... | collective-permute-start | bytes 294920 | tf_op jit(solution)/shard_map/ppermute | solution.py:378
where the time goes:
time: 11.9 us; the launch traced here: 11.8 us
  Pallas kernels  7.04 us (59%)
  other arithmetic  2 us (17%)
  starting transfers between devices  1.86 us (16%)
  waiting for transfers between devices  0.86 us (7%)
    pallas_call x1, Pallas kernels, body(): pl.pallas_call(lambda *refs: kernel(cells, tiles, *refs), out_shape=shape...  4.53 us
    pallas_call x1, Pallas kernels, body(): pl.pallas_call(lambda *refs: prepare(cells, tiles, *refs), out_shape=(sha...  2.51 us
    ppermute x1, starting transfers between devices, body(): left = lax.ppermute(both[:, cells - HALO:], 'lon', ring)  1.85 us
    concatenate x1, other arithmetic, body(): jnp.concatenate([start.reshape(-1, lat_cells), depth, table], axis=0)  1 us
    concatenate x1, other arithmetic, body(): both = jnp.concatenate([start, depth[None]], axis=0)  1 us
    ppermute x1, waiting for transfers between devices, body(): right = lax.ppermute(both[:, :HALO], 'lon', [(j, i) for i, j in ring])  0.86 us
  transfers between devices with their start and end apart: 2, of which 1 were waited for; matrix products, arithmetic and copies ran while one was open for 8% of the time, Pallas kernels for 21%

commit v1 on v0

--- a/solution.py
+++ b/solution.py
@@ -22,6 +22,7 @@
 DEAL_ROWS = 64
 FIRST, MORE = 3, 4
 VMEM_LIMIT = 24 << 20
+EDGE_LIMIT = 2 << 20
 
 EAST, POLE, DIVERGE, SPIN_U, SPIN_V, GRAD_E, GRAD_N, TURN_C, TURN_U, TURN_V, EAST_INV, POLE_INV = range(12)
 
@@ -221,6 +222,16 @@
     lax.fori_loop(0, (number + MORE - FIRST - 1) // MORE, more, 0)
 
 
+def cut_edges(cells, stacked, outer, inner):
+    odd = lax.axis_index("lon") % 2 == 1
+    for field in range(4):
+        low = stacked[field * cells : field * cells + HALO, :]
+        high = stacked[(field + 1) * cells - HALO : (field + 1) * cells, :]
+        rows = slice(field * HALO, (field + 1) * HALO)
+        outer[rows, :] = jnp.where(odd, high, low)
+        inner[rows, :] = jnp.where(odd, low, high)
+
+
 def prepare(cells, tiles, stacked, out, table, dealing, undealing, inner, joint, *scratch):
     number = lax.axis_index("tm")
     for row in range(table.shape[0]):
@@ -275,7 +286,7 @@
     in_blocks(number, one_block)
 
 
-def kernel(cells, tiles, own, left, right, table, dealing, undealing, inner, joint, ends, *scratch):
+def kernel(cells, tiles, own, outer_halo, inner_halo, table, dealing, undealing, inner, joint, ends, *scratch):
     (s_h, grad_e, grad_n, w_h, w_a, w_b, firsts, flat) = scratch[:8]
     guesses = [scratch[8 + 2 * k : 10 + 2 * k] for k in range(MORE)]
     temps_of = streams_of(scratch[8 + 2 * MORE :])
@@ -285,10 +296,10 @@
     fluid = Fluid(table, tiles, grad_e, grad_n)
 
     fields = (s_h, *guesses[0], grad_e, grad_n)
-    for side, halo in enumerate((left, right)):
-        for field in range(4):
-            first_row = (4 * side + field) * HALO
-            flat[first_row : first_row + HALO, :] = halo[field]
+    odd = lax.axis_index("lon") % 2 == 1
+    far, near = outer_halo[...], inner_halo[...]
+    flat[: 4 * HALO, :] = jnp.where(odd, near, far)
+    flat[4 * HALO :, :] = jnp.where(odd, far, near)
     dealt = times_one_hot(flat[...], dealing[...])
     put_fields(dealt, table, tiles, HALO, 0, HALO, fields, 0)
     put_fields(dealt, table, tiles, HALO, 4 * HALO, HALO, fields, HALO + cells)
@@ -372,14 +383,22 @@
     tiles = lat_cells // LANES
     slots = FIRST + MORE * (max(lax.axis_size("tm") - 1 - FIRST + MORE - 1, 0) // MORE)
     table = jnp.asarray(lat_table(cells * count, lat_cells))
-    both = jnp.concatenate([start, depth[None]], axis=0)
-    ring = [(i, (i + 1) % count) for i in range(count)]
-    left = lax.ppermute(both[:, cells - HALO :], "lon", ring)
-    right = lax.ppermute(both[:, :HALO], "lon", [(j, i) for i, j in ring])
     stacked = jnp.concatenate([start.reshape(-1, lat_cells), depth, table], axis=0)
+    vmem = pl.BlockSpec(memory_space=pltpu.VMEM)
+    side = jax.ShapeDtypeStruct((4 * HALO, lat_cells), jnp.float32)
+    outer, inner = pl.pallas_call(
+        lambda *refs: cut_edges(cells, *refs),
+        out_shape=(side, side),
+        in_specs=[vmem],
+        out_specs=[vmem] * 2,
+        compiler_params=pltpu.CompilerParams(vmem_limit_bytes=EDGE_LIMIT),
+        name="edges",
+    )(stacked)
+    ring = range(count)
+    outer = lax.ppermute(outer, "lon", [(k, (k + 1 if k % 2 else k - 1) % count) for k in ring])
+    inner = lax.ppermute(inner, "lon", [(k, k ^ 1) for k in ring])
     wide = cells + 2 * HALO
     inside = -(-(cells - 4 * STEPS) // ROWS) * ROWS
-    vmem = pl.BlockSpec(memory_space=pltpu.VMEM)
 
     def shape(*dims, dtype=jnp.float32):
         return jax.ShapeDtypeStruct(dims, dtype)
@@ -417,7 +436,7 @@
         + [scratch(tiles, wide, LANES)] * (9 * MORE),
         compiler_params=params,
         name="parareal",
-    )(prepared[0], left, right, *prepared[1:])
+    )(prepared[0], outer, inner, *prepared[1:])
 
 
 def solution(mesh):

time: 11.9 us -> 11.1 us (0.933)
  other arithmetic: 2 us -> 1 us
  waiting for transfers between devices: 0.86 us -> 0.98 us
    concatenate x1 -> x0, other arithmetic: 1 us -> none  [body(): both = jnp.concatenate([start, depth[None]], axis=0)]
    ppermute x2, waiting for transfers between devices: 0.86 us -> 0.98 us  [the longest x1 0.98 us: body(): lax.ppermute(outer, 'lon', [(k, (k + 1 if k % 2 else k - 1) % count) for...]
  transfers between devices with their start and end apart: 2 -> 2, of which waited for: 1 -> 1; matrix products, arithmetic and copies ran while one was open for 8% -> 0% of each run, Pallas kernels for 21% -> 23%
where the time goes in v1:
time: 11.1 us; the launch traced here: 10.9 us
  Pallas kernels  7.06 us (64%)
  starting transfers between devices  1.87 us (17%)
  other arithmetic  1 us (9%)
  waiting for transfers between devices  0.98 us (9%)
    pallas_call x1, Pallas kernels, body(): pl.pallas_call(lambda *refs: kernel(cells, tiles, *refs), out_shape=shape...  4.5 us
    pallas_call x1, Pallas kernels, body(): pl.pallas_call(lambda *refs: prepare(cells, tiles, *refs), out_shape=(sha...  2.51 us
    ppermute x1, starting transfers between devices, body(): lax.ppermute(outer, 'lon', [(k, (k + 1 if k % 2 else k - 1) % count) for...  1.87 us
    concatenate x1, other arithmetic, body(): jnp.concatenate([start.reshape(-1, lat_cells), depth, table], axis=0)  1 us
    ppermute x1, waiting for transfers between devices, body(): lax.ppermute(outer, 'lon', [(k, (k + 1 if k % 2 else k - 1) % count) for...  0.98 us
  transfers between devices with their start and end apart: 2, of which 1 were waited for; matrix products, arithmetic and copies ran while one was open for 0% of the time, Pallas kernels for 23%

profile of v1, /device:TPU:27, one launch (start us, length us, event | category | flops | bytes accessed | tf_op | source)
XLA Modules:
  0.0 10.9 jit_solution(12482923185578795641)
XLA Ops:
  0.0 1.0 %pad_maximum_fusion.refs_0_ = f32[140,512]{1,0:T(8,128)S(1)} fusion(f32[12,512]{1,0:T(8,128)} %constant.2.clone, f32[32,512]{1,0:T(8,128)} %param.4, f32[96,512]{1,0:T(8,128)} %bitcast.1), kind=kLoop, calls=%fused_computation | loop fusion | flops 143360 | bytes 573440 | tf_op jit(solution)/shard_map/concatenate | solution.py:386
  1.1 1.9 %collective-permute-start = (f32[48,512]{1,0:T(8,128)S(1)}, f32[48,512]{1,0:T(8,128)S(1)}, u32[]{:S(2)}, u32[]{:S(2)}) collective-permute-start(f32[48,512]{1,0:T(8,128)S(1)} %get-tuple-element.14), channel_id=1, source_target_pairs={{0,3},{1,2},{2,1},{3,0},{4,7},{5,6},{6,5},{7,4},{8,11},{9,10},{10,... | collective-permute-start | bytes 294920 | tf_op jit(solution)/shard_map/ppermute | solution.py:398
  2.9 0.0 collective-permute-start.1
  2.9 2.5 %prepare.1 = (f32[7,4,32,128]{3,2,1,0:T(8,128)S(1)}, f32[12,8,512]{2,1,0:T(8,128)S(1)}, bf16[512,512]{1,0:T(8,128)(2,1)S(1)}, bf16[512,512]{1,0:T(8,128)(2,1)S(1...) custom-call(f32[140,512]{1,0:T(8,128)S(1)} %pad_maximum_fusion.refs_0_), custom_call_target="tpu_custom_call" | custom-call | flops 1000000000 | bytes 10000000 | tf_op jit(solution)/shard_map/prepare/pallas_call | solution.py:412
  5.4 1.0 %collective-permute-done.refs_1_ = f32[48,512]{1,0:T(8,128)S(1)} collective-permute-done((f32[48,512]{1,0:T(8,128)S(1)}, f32[48,512]{1,0:T(8,128)S(1)}, u32[]{:S(2)}, u32[]{:S(2)}) %collective-permute-start) | collective-permute-done | bytes 98336 | tf_op jit(solution)/shard_map/ppermute | solution.py:398
  6.4 0.0 collective-permute-done.1.refs_2_
  6.4 4.5 %parareal.1 = f32[1,3,32,512]{3,2,1,0:T(8,128)} custom-call(f32[7,4,32,128]{3,2,1,0:T(8,128)S(1)} %get-tuple-element.13.refs_0_, f32[48,512]{1,0:T(8,128)S(1)} %collective-permute-done.refs_1_, f32[48,512]{1,0:T(8,128)S(1)} %collective-permute-done.1.refs_2_, f32[12,8,512]{2,1,0:T(8,128)S(1)} %get-tuple-element.16.refs_3_, ...), custom_call_target="tpu_custom_call" | custom-call | tf_op jit(solution)/shard_map/parareal/pallas_call | solution.py:429
  (1 shorter events, 0.0 us)
Async XLA Ops:
  1.1 5.4 %collective-permute-start = (f32[48,512]{1,0:T(8,128)S(1)}, f32[48,512]{1,0:T(8,128)S(1)}, u32[]{:S(2)}, u32[]{:S(2)}) collective-permute-start(f32[48,512]{1,0:T(8,128)S(1)} %get-tuple-element.14), channel_id=1, source_target_pairs={{0,3},{1,2},{2,1},{3,0},{4,7},{5,6},{6,5},{7,4},{8,11},{9,10},{10,... | collective-permute-start | bytes 294920 | tf_op jit(solution)/shard_map/ppermute | solution.py:398
  2.9 3.5 %collective-permute-start.1 = (f32[48,512]{1,0:T(8,128)S(1)}, f32[48,512]{1,0:T(8,128)S(1)}, u32[]{:S(2)}, u32[]{:S(2)}) collective-permute-start(f32[48,512]{1,0:T(8,128)S(1)} %get-tuple-element.15), channel_id=1, source_target_pairs={{0,1},{1,0},{2,3},{3,2},{4,5},{5,4},{6,7},{7,6},{8,9},{9,8},{10,11... | collective-permute-start | bytes 294920 | tf_op jit(solution)/shard_map/ppermute | solution.py:399

commit v2 on v1

--- a/solution.py
+++ b/solution.py
@@ -20,7 +20,7 @@
 ROWS = 8
 LANES = 128
 DEAL_ROWS = 64
-FIRST, MORE = 3, 4
+FIRST, MORE, ABREAST = 3, 4, 7
 VMEM_LIMIT = 24 << 20
 EDGE_LIMIT = 2 << 20
 
@@ -95,6 +95,51 @@
     return slice(t * LANES, (t + 1) * LANES)
 
 
+def field_values(part, table, t):
+    h, u, v, d = part
+    he = d * table[EAST, :1, lanes(t)]
+    hp = d * table[POLE, :1, lanes(t)]
+    return h, u * he, v * hp, he * table[GRAD_E, :1, lanes(t)], hp * table[GRAD_N, :1, lanes(t)]
+
+
+def windows(low, high):
+    starts = list(range(low, high - ROWS + 1, ROWS))
+    if starts[-1] + ROWS < high:
+        starts.append(high - ROWS)
+    return starts
+
+
+def deal(tiles, dealing, undealing):
+    def block(index, carry):
+        start = pl.multiple_of(index * DEAL_ROWS, DEAL_ROWS)
+        row = start + lax.broadcasted_iota(jnp.int32, (DEAL_ROWS, LANES), 0)
+        lane = lax.broadcasted_iota(jnp.int32, (DEAL_ROWS, LANES), 1)
+        place = row % LANES * tiles + row // LANES
+        for t in range(tiles):
+            hit = row == lane * tiles + t
+            dealing[pl.ds(start, DEAL_ROWS), lanes(t)] = jnp.where(hit, 1.0, 0.0).astype(jnp.bfloat16)
+            hit = place == lane + t * LANES
+            undealing[pl.ds(start, DEAL_ROWS), lanes(t)] = jnp.where(hit, 1.0, 0.0).astype(jnp.bfloat16)
+        return carry
+
+    lax.fori_loop(0, tiles * LANES // DEAL_ROWS, block, 0)
+
+
+def times_one_hot(values, matrix):
+    pieces = []
+    rest = values
+    for _ in range(3):
+        pieces.append(rest.astype(jnp.bfloat16))
+        rest = rest - pieces[-1].astype(jnp.float32)
+    count = values.shape[0]
+    out = jnp.dot(jnp.concatenate(pieces, axis=0), matrix, preferred_element_type=jnp.float32)
+    return out[:count] + out[count : 2 * count] + out[2 * count :]
+
+
+def lanes(t):
+    return slice(t * LANES, (t + 1) * LANES)
+
+
 def put_fields(dealt, table, tiles, count, first_row, step, refs, base):
     for t in range(tiles):
         h, u, v, d = (
@@ -122,13 +167,14 @@
     ]
 
 
-def strips(wide):
+def strip(wide, is_left):
     offsets = range(0, HALO, ROWS)
+
+    def pick(first, k):
+        return jnp.where(is_left, first + k, wide - first - ROWS - k)
+
     return [
-        (
-            [2 * s - 1 + k for k in offsets] + [wide - 2 * s + 1 - ROWS - k for k in offsets],
-            [2 * s + k for k in offsets] + [wide - 2 * s - ROWS - k for k in offsets],
-        )
+        ([pick(2 * s - 1, k) for k in offsets], [pick(2 * s, k) for k in offsets])
         for s in range(1, STEPS + 1)
     ]
 
@@ -138,11 +184,11 @@
 
 
 def at(ref, t, row):
-    return ref[t, row : row + ROWS, :]
+    return ref[t, pl.ds(row, ROWS), :]
 
 
 def put(ref, t, row, value):
-    ref[t, row : row + ROWS, :] = value
+    ref[t, pl.ds(row, ROWS), :] = value
 
 
 class Fluid:
@@ -181,7 +227,7 @@
                     value = at(height, t, row) - (at(alpha, t, row + 1) - at(alpha, t, row - 1))
                     put(new_h, t, row, value - diverge[t] * flux[t])
             spin_u, spin_v = self.consts(SPIN_U, SPIN_V)
-            for row in rest_rows:
+            for index, row in enumerate(rest_rows):
                 here = [at(new_h, t, row) for t in tiles]
                 slope = self.north_diff(here)
                 for t in tiles:
@@ -190,11 +236,34 @@
                     a = at(alpha, t, row) + spin_u[t] * b - at(self.grad_e, t, row) * east
                     b = b - spin_v[t] * a - at(self.grad_n, t, row) * slope[t]
                     if step == STEPS - 1:
-                        finish(t, row, here[t], a, b)
+                        finish(index, t, row, here[t], a, b)
                     else:
                         put(new_a, t, row, a)
                         put(new_b, t, row, b)
             state = (new_h, new_a, new_b)
+
+    def next_first(self, m, firsts, out, guess, is_left=None):
+        before = [firsts.at[m, field] for field in range(3)]
+        after = [firsts.at[m + 1, field] for field in range(3)]
+        sublane = lax.broadcasted_iota(jnp.int32, (ROWS, LANES), 0)
+        spare = HALO % ROWS
+        outward = None
+        if is_left is not None and spare:
+            outward = jnp.where(is_left, sublane, ROWS - 1 - sublane) < spare
+
+        def finish(index, t, row, h, a, b):
+            da, db = self.turn(
+                at(before[1], t, row) - at(guess[0], t, row),
+                at(before[2], t, row) - at(guess[1], t, row),
+                t,
+            )
+            values = (h + (at(before[0], t, row) - at(out.at[0], t, row)), a + da, b + db)
+            for ref, value in zip(after, values):
+                if outward is not None and (index + 1) * ROWS > HALO:
+                    value = jnp.where(outward, value, at(ref, t, row))
+                put(ref, t, row, value)
+
+        return finish
 
     def turn_rows(self, source, target, rows):
         for row in rows:
@@ -212,14 +281,14 @@
     return [stages(refs[7 * k : 7 * k + 7]) for k in range(len(refs) // 7)]
 
 
-def in_blocks(number, one_block):
-    one_block(0, FIRST)
-
-    def more(index, carry):
-        one_block(FIRST + MORE * index, MORE)
+def in_blocks(number, one_block, first, more):
+    one_block(0, first)
+
+    def rest(index, carry):
+        one_block(first + more * index, more)
         return carry
 
-    lax.fori_loop(0, (number + MORE - FIRST - 1) // MORE, more, 0)
+    lax.fori_loop(0, (number + more - first - 1) // more, rest, 0)
 
 
 def cut_edges(cells, stacked, outer, inner):
@@ -232,120 +301,115 @@
         inner[rows, :] = jnp.where(odd, low, high)
 
 
-def prepare(cells, tiles, stacked, out, table, dealing, undealing, inner, joint, *scratch):
+def prepare(cells, tiles, stacked, out, scales, table, dealing, undealing, firsts, joint, *scratch):
     number = lax.axis_index("tm")
     for row in range(table.shape[0]):
         source = stacked[4 * cells + row : 4 * cells + row + 1, :]
         table[row] = jnp.broadcast_to(source, (ROWS, tiles * LANES))
     deal(tiles, dealing, undealing)
     dealt = times_one_hot(stacked[: 4 * cells, :], dealing[...])
-    put_fields(dealt, table, tiles, cells, 0, cells, [out.at[k] for k in range(5)], 0)
     for t in range(tiles):
-        over = 1.0 / dealt[3 * cells :, lanes(t)]
-        out[5, t] = over * table[EAST_INV, :1, lanes(t)]
-        out[6, t] = over * table[POLE_INV, :1, lanes(t)]
+        part = [dealt[f * cells : (f + 1) * cells, lanes(t)] for f in range(4)]
+        for field, value in enumerate(field_values(part, table, t)):
+            out[field, t, HALO : HALO + cells, :] = value
+            if field < 3:
+                firsts[0, field, t, HALO : HALO + cells, :] = value
+        over = 1.0 / part[3]
+        scales[0, t] = over * table[EAST_INV, :1, lanes(t)]
+        scales[1, t] = over * table[POLE_INV, :1, lanes(t)]
 
     fluid = Fluid(table, tiles, out.at[3], out.at[4])
-    reach = 2 * STEPS
-    plan = shrinking(0, cells)
+    plan = shrinking(HALO, HALO + cells)
     guesses = [scratch[2 * k : 2 * k + 2] for k in range(MORE)]
     temps_of = streams_of(scratch[2 * MORE :])
     guesses[0][0][...] = out[1]
     guesses[0][1][...] = out[2]
-    for field in range(3):
-        inner[0, field, :, : cells - 2 * reach, :] = out[field, :, reach : cells - reach, :]
-    every = range(0, cells, ROWS)
+    every = range(HALO, HALO + cells, ROWS)
 
     def one_block(start, count):
         for k in range(count):
-            one_slice(start + k, guesses[k], temps_of[k])
+            m, temps = start + k, temps_of[k]
+            fluid.fine((out.at[0], *guesses[k]), temps, plan, fluid.next_first(m, firsts, out, guesses[k]))
+            for step, sides in enumerate(joints(HALO, HALO + cells)):
+                for side, row in enumerate(sides):
+                    for field in range(3):
+                        for t in range(tiles):
+                            joint[m, step, side, field, t] = at(temps[step][field], t, row)
             fluid.turn_rows(guesses[k], guesses[(k + 1) % count], every)
 
-    def one_slice(m, guess, temps):
-        before = [inner.at[m, field] for field in range(3)]
-        after = [inner.at[m + 1, field] for field in range(3)]
-
-        def finish(t, row, h, a, b):
-            own_row = row - reach
-            put(after[0], t, own_row, h + (at(before[0], t, own_row) - out[0, t, row : row + ROWS, :]))
-            da, db = fluid.turn(
-                at(before[1], t, own_row) - at(guess[0], t, row),
-                at(before[2], t, own_row) - at(guess[1], t, row),
-                t,
-            )
-            put(after[1], t, own_row, a + da)
-            put(after[2], t, own_row, b + db)
-
-        fluid.fine((out.at[0], *guess), temps, plan, finish)
-        for step, sides in enumerate(joints(0, cells)):
-            for side, row in enumerate(sides):
+    in_blocks(number, one_block, FIRST, MORE)
+
+
+def one_side(cells, tiles, is_left, halo, table, dealing, out, firsts, joint, flat, guesses, temps_of):
+    wide = cells + 2 * HALO
+    number = lax.axis_index("tm")
+    fluid = Fluid(table, tiles, out.at[3], out.at[4])
+    dealt = times_one_hot(halo[...], dealing[...])
+    for t in range(tiles):
+        flat[t] = dealt[:, lanes(t)]
+    base = jnp.where(is_left, 0, HALO + cells)
+    for row in windows(0, HALO):
+        for t in range(tiles):
+            part = [at(flat, t, f * HALO + row) for f in range(4)]
+            for field, value in enumerate(field_values(part, table, t)):
+                put(out.at[field], t, base + row, value)
+                if field < 3:
+                    put(firsts.at[0, field], t, base + row, value)
+    plan = strip(wide, is_left)
+    near = [jnp.where(is_left, k, wide - ROWS - k) for k in range(0, HALO + ROWS, ROWS)]
+    for row in near:
+        for t in range(tiles):
+            for field in range(2):
+                put(guesses[0][field], t, row, at(out.at[1 + field], t, row))
+    side = jnp.where(is_left, 0, 1)
+    left_joints = joints(HALO, HALO + cells)
+
+    def one_block(start, count):
+        for k in range(count):
+            m, temps = start + k, temps_of[k]
+            for step, (row_left, row_right) in enumerate(left_joints):
+                row = jnp.where(is_left, row_left, row_right)
                 for field in range(3):
                     for t in range(tiles):
-                        joint[m, step, side, field, t] = at(temps[step][field], t, row)
-
-    in_blocks(number, one_block)
-
-
-def kernel(cells, tiles, own, outer_halo, inner_halo, table, dealing, undealing, inner, joint, ends, *scratch):
-    (s_h, grad_e, grad_n, w_h, w_a, w_b, firsts, flat) = scratch[:8]
-    guesses = [scratch[8 + 2 * k : 10 + 2 * k] for k in range(MORE)]
-    temps_of = streams_of(scratch[8 + 2 * MORE :])
+                        put(temps[step][field], t, row, joint[m, step, side, field, t])
+            fluid.fine(
+                (out.at[0], *guesses[k]), temps, plan, fluid.next_first(m, firsts, out, guesses[k], is_left)
+            )
+            fluid.turn_rows(guesses[k], guesses[(k + 1) % count], near)
+
+    in_blocks(number, one_block, ABREAST, MORE)
+
+
+def near_side(cells, tiles, halo, table, dealing, joint, out_in, firsts_in, out, firsts, *scratch):
+    is_left = lax.axis_index("lon") % 2 == 1
+    guesses = [scratch[1 + 2 * k : 3 + 2 * k] for k in range(ABREAST)]
+    temps_of = streams_of(scratch[1 + 2 * ABREAST :])
+    one_side(
+        cells, tiles, is_left, halo, table, dealing, out, firsts, joint, scratch[0], guesses, temps_of
+    )
+
+
+def kernel(
+    cells, tiles, halo, table, dealing, undealing, scales, joint, out_in, firsts_in,
+    ends, out, firsts, *scratch,
+):
+    is_left = lax.axis_index("lon") % 2 == 0
+    w_h, w_a, w_b = scratch[1:4]
+    guesses = [scratch[4 + 2 * k : 6 + 2 * k] for k in range(ABREAST)]
+    temps_of = streams_of(scratch[4 + 2 * ABREAST :])
     wide = cells + 2 * HALO
     reach = 2 * STEPS
     number = lax.axis_index("tm")
-    fluid = Fluid(table, tiles, grad_e, grad_n)
-
-    fields = (s_h, *guesses[0], grad_e, grad_n)
-    odd = lax.axis_index("lon") % 2 == 1
-    far, near = outer_halo[...], inner_halo[...]
-    flat[: 4 * HALO, :] = jnp.where(odd, near, far)
-    flat[4 * HALO :, :] = jnp.where(odd, far, near)
-    dealt = times_one_hot(flat[...], dealing[...])
-    put_fields(dealt, table, tiles, HALO, 0, HALO, fields, 0)
-    put_fields(dealt, table, tiles, HALO, 4 * HALO, HALO, fields, HALO + cells)
-    for k, ref in enumerate(fields):
-        ref[:, HALO : HALO + cells, :] = own[k]
-    for field, ref in enumerate(fields[:3]):
-        firsts[0, field] = ref[...]
-
-    edge_rows = [*range(0, HALO + ROWS, ROWS)]
-    edge_rows = sorted({*edge_rows, *(wide - ROWS - row for row in edge_rows)})
-
-    def round_one(m, guess, temps):
-        before = [firsts.at[m, field] for field in range(3)]
-        after = [firsts.at[m + 1, field] for field in range(3)]
-
-        def finish(t, row, h, a, b):
-            put(after[0], t, row, h + (at(before[0], t, row) - at(s_h, t, row)))
-            da, db = fluid.turn(
-                at(before[1], t, row) - at(guess[0], t, row),
-                at(before[2], t, row) - at(guess[1], t, row),
-                t,
-            )
-            put(after[1], t, row, a + da)
-            put(after[2], t, row, b + db)
-
-        for step, sides in enumerate(joints(HALO, HALO + cells)):
-            for side, row in enumerate(sides):
-                for field in range(3):
-                    for t in range(tiles):
-                        put(temps[step][field], t, row, joint[m, step, side, field, t])
-        fluid.fine((s_h, *guess), temps, strips(wide), finish)
-        for row in windows(0, cells - 2 * reach):
-            for field in range(3):
-                for t in range(tiles):
-                    put(after[field], t, HALO + reach + row, at(inner.at[m + 1, field], t, row))
-
-    def block_one(start, count):
-        for k in range(count):
-            round_one(start + k, guesses[k], temps_of[k])
-            fluid.turn_rows(guesses[k], guesses[(k + 1) % count], edge_rows)
+    fluid = Fluid(table, tiles, out.at[3], out.at[4])
+    one_side(
+        cells, tiles, is_left, halo, table, dealing, out, firsts, joint, scratch[0], guesses, temps_of
+    )
 
     def round_two(m, temps):
         first = [firsts.at[m, field] for field in range(3)]
         active = m <= number
 
-        def finish(t, row, h, a, b):
+        def finish(step_row, t, row, h, a, b):
             wh, wa, wb = (at(ref, t, row) for ref in (w_h, w_a, w_b))
             da, db = fluid.turn(wa - at(first[1], t, row), wb - at(first[2], t, row), t)
             put(w_h, t, row, jnp.where(active, h + (wh - at(first[0], t, row)), wh))
@@ -358,19 +422,18 @@
         for k in range(count):
             round_two(1 + start + k, temps_of[k])
 
-    in_blocks(number, block_one)
     for field, ref in enumerate((w_h, w_a, w_b)):
         ref[...] = firsts[1, field]
 
     @pl.when(number > 0)
     def _():
-        in_blocks(number, block_two)
+        in_blocks(number, block_two, FIRST, MORE)
 
     rows = slice(HALO, HALO + cells)
     whole = [
         jnp.concatenate([w_h[t, rows, :] for t in range(tiles)], axis=1),
-        jnp.concatenate([w_a[t, rows, :] * own[5, t] for t in range(tiles)], axis=1),
-        jnp.concatenate([w_b[t, rows, :] * own[6, t] for t in range(tiles)], axis=1),
+        jnp.concatenate([w_a[t, rows, :] * scales[0, t] for t in range(tiles)], axis=1),
+        jnp.concatenate([w_b[t, rows, :] * scales[1, t] for t in range(tiles)], axis=1),
     ]
     whole = times_one_hot(jnp.concatenate(whole, axis=0), undealing[...])
     for field in range(3):
@@ -381,7 +444,8 @@
     count = lax.axis_size("lon")
     _, cells, lat_cells = start.shape
     tiles = lat_cells // LANES
-    slots = FIRST + MORE * (max(lax.axis_size("tm") - 1 - FIRST + MORE - 1, 0) // MORE)
+    last = lax.axis_size("tm") - 1
+    slots = max(first + MORE * max(-(-(last - first) // MORE), 0) for first in (FIRST, ABREAST))
     table = jnp.asarray(lat_table(cells * count, lat_cells))
     stacked = jnp.concatenate([start.reshape(-1, lat_cells), depth, table], axis=0)
     vmem = pl.BlockSpec(memory_space=pltpu.VMEM)
@@ -398,7 +462,6 @@
     outer = lax.ppermute(outer, "lon", [(k, (k + 1 if k % 2 else k - 1) % count) for k in ring])
     inner = lax.ppermute(inner, "lon", [(k, k ^ 1) for k in ring])
     wide = cells + 2 * HALO
-    inside = -(-(cells - 4 * STEPS) // ROWS) * ROWS
 
     def shape(*dims, dtype=jnp.float32):
         return jax.ShapeDtypeStruct(dims, dtype)
@@ -406,37 +469,50 @@
     def scratch(*dims):
         return pltpu.VMEM(dims, jnp.float32)
 
-    params = pltpu.CompilerParams(
-        vmem_limit_bytes=VMEM_LIMIT
-    )
-    prepared = pl.pallas_call(
+    params = pltpu.CompilerParams(vmem_limit_bytes=VMEM_LIMIT)
+    block = scratch(tiles, wide, LANES)
+    fields = shape(5, tiles, wide, LANES)
+    firsts = shape(slots + 1, 3, tiles, wide, LANES)
+    halo = scratch(tiles, 4 * HALO, LANES)
+    fields, scales, table, dealing, undealing, firsts, joint = pl.pallas_call(
         lambda *refs: prepare(cells, tiles, *refs),
         out_shape=(
-            shape(7, tiles, cells, LANES),
+            fields,
+            shape(2, tiles, cells, LANES),
             shape(table.shape[0], ROWS, lat_cells),
             shape(lat_cells, lat_cells, dtype=jnp.bfloat16),
             shape(lat_cells, lat_cells, dtype=jnp.bfloat16),
-            shape(slots + 1, 3, tiles, inside, LANES),
+            firsts,
             shape(slots, STEPS - 1, 2, 3, tiles, ROWS, LANES),
         ),
         in_specs=[vmem],
-        out_specs=[vmem] * 6,
-        scratch_shapes=[scratch(tiles, cells, LANES)] * (9 * MORE),
+        out_specs=[vmem] * 7,
+        scratch_shapes=[block] * (9 * MORE),
         compiler_params=params,
         cost_estimate=pl.CostEstimate(flops=10**9, bytes_accessed=10**7, transcendentals=0),
         name="prepare",
     )(stacked)
+    fields, firsts = pl.pallas_call(
+        lambda *refs: near_side(cells, tiles, *refs),
+        out_shape=(shape(*fields.shape), shape(*firsts.shape)),
+        in_specs=[vmem] * 6,
+        out_specs=[vmem] * 2,
+        scratch_shapes=[halo] + [block] * (9 * ABREAST),
+        input_output_aliases={4: 0, 5: 1},
+        compiler_params=params,
+        cost_estimate=pl.CostEstimate(flops=10**9, bytes_accessed=10**7, transcendentals=0),
+        name="near",
+    )(inner, table, dealing, joint, fields, firsts)
     return pl.pallas_call(
         lambda *refs: kernel(cells, tiles, *refs),
-        out_shape=shape(1, *start.shape),
+        out_shape=(shape(1, *start.shape), shape(*fields.shape), shape(*firsts.shape)),
         in_specs=[vmem] * 8,
-        out_specs=vmem,
-        scratch_shapes=[scratch(tiles, wide, LANES)] * 6
-        + [scratch(slots + 1, 3, tiles, wide, LANES), scratch(8 * HALO, lat_cells)]
-        + [scratch(tiles, wide, LANES)] * (9 * MORE),
+        out_specs=[vmem] * 3,
+        scratch_shapes=[halo] + [block] * (3 + 9 * ABREAST),
+        input_output_aliases={6: 1, 7: 2},
         compiler_params=params,
         name="parareal",
-    )(prepared[0], outer, inner, *prepared[1:])
+    )(outer, table, dealing, undealing, scales, joint, fields, firsts)[0]
 
 
 def solution(mesh):

time: 11.1 us -> 10.7 us (0.964)
  waiting for transfers between devices: 0.98 us -> 0.01 us
  Pallas kernels: 7.06 us -> 7.58 us
    ppermute x1, waiting for transfers between devices: 0.98 us -> 0.01 us  [body(): lax.ppermute(outer, 'lon', [(k, (k + 1 if k % 2 else k - 1) % count) for...]
    ppermute x1, starting transfers between devices: 0.01 us -> 0.74 us  [body(): inner = lax.ppermute(inner, 'lon', [(k, k ^ 1) for k in ring])]
    ppermute x1, starting transfers between devices: 1.87 us -> 1.2 us  [body(): lax.ppermute(outer, 'lon', [(k, (k + 1 if k % 2 else k - 1) % count) for...]
    pallas_call x2 -> x3, Pallas kernels: 7.01 us -> 7.53 us  [the longest x1 3.84 us: body(): pl.pallas_call(lambda *refs: kernel(cells, tiles, *refs), out_shape=(shap...]
  transfers between devices with their start and end apart: 2 -> 2, of which waited for: 1 -> 0; matrix products, arithmetic and copies ran while one was open for 0% -> 0% of each run, Pallas kernels for 23% -> 35%
where the time goes in v2:
time: 10.7 us; the launch traced here: 10.6 us
  Pallas kernels  7.58 us (71%)
  starting transfers between devices  1.94 us (18%)
  other arithmetic  1 us (9%)
    pallas_call x1, Pallas kernels, body(): pl.pallas_call(lambda *refs: kernel(cells, tiles, *refs), out_shape=(shap...  3.84 us
    pallas_call x1, Pallas kernels, body(): pl.pallas_call(lambda *refs: prepare(cells, tiles, *refs), out_shape=(fie...  2.36 us
    pallas_call x1, Pallas kernels, body(): pl.pallas_call(lambda *refs: near_side(cells, tiles, *refs), out_shape=(s...  1.33 us
    ppermute x1, starting transfers between devices, body(): lax.ppermute(outer, 'lon', [(k, (k + 1 if k % 2 else k - 1) % count) for...  1.2 us
    concatenate x1, other arithmetic, body(): jnp.concatenate([start.reshape(-1, lat_cells), depth, table], axis=0)  1 us
    ppermute x1, starting transfers between devices, body(): inner = lax.ppermute(inner, 'lon', [(k, k ^ 1) for k in ring])  0.74 us
  transfers between devices with their start and end apart: 2, of which 0 were waited for; matrix products, arithmetic and copies ran while one was open for 0% of the time, Pallas kernels for 35%

profile of v2, /device:TPU:27, one launch (start us, length us, event | category | flops | bytes accessed | tf_op | source)
XLA Modules:
  0.0 10.6 jit_solution(5457552562883527101)
XLA Ops:
  0.0 1.0 %pad_maximum_fusion.refs_0_ = f32[140,512]{1,0:T(8,128)S(1)} fusion(f32[12,512]{1,0:T(8,128)} %constant.2.clone, f32[32,512]{1,0:T(8,128)} %param.4, f32[96,512]{1,0:T(8,128)} %bitcast.1), kind=kLoop, calls=%fused_computation | loop fusion | flops 143360 | bytes 573440 | tf_op jit(solution)/shard_map/concatenate | solution.py:450
  1.1 0.7 %collective-permute-start.1 = (f32[48,512]{1,0:T(8,128)S(1)}, f32[48,512]{1,0:T(8,128)S(1)}, u32[]{:S(2)}, u32[]{:S(2)}) collective-permute-start(f32[48,512]{1,0:T(8,128)S(1)} %get-tuple-element.23), channel_id=1, source_target_pairs={{0,1},{1,0},{2,3},{3,2},{4,5},{5,4},{6,7},{7,6},{8,9},{9,8},{10,11... | collective-permute-start | bytes 294920 | tf_op jit(solution)/shard_map/ppermute | solution.py:463
  1.8 1.2 %collective-permute-start = (f32[48,512]{1,0:T(8,128)S(1)}, f32[48,512]{1,0:T(8,128)S(1)}, u32[]{:S(2)}, u32[]{:S(2)}) collective-permute-start(f32[48,512]{1,0:T(8,128)S(1)} %get-tuple-element.17), channel_id=1, source_target_pairs={{0,3},{1,2},{2,1},{3,0},{4,7},{5,6},{6,5},{7,4},{8,11},{9,10},{10,... | collective-permute-start | bytes 294920 | tf_op jit(solution)/shard_map/ppermute | solution.py:462
  3.0 2.4 %prepare.1 = (f32[5,4,56,128]{3,2,1,0:T(8,128)S(1)}, f32[2,4,32,128]{3,2,1,0:T(8,128)S(1)}, f32[12,8,512]{2,1,0:T(8,128)S(1)}, bf16[512,512]{1,0:T(8,128)(2,1)S(...) custom-call(f32[140,512]{1,0:T(8,128)S(1)} %pad_maximum_fusion.refs_0_), custom_call_target="tpu_custom_call" | custom-call | flops 1000000000 | bytes 10000000 | tf_op jit(solution)/shard_map/prepare/pallas_call | solution.py:477
  5.4 0.0 collective-permute-done.1.refs_0_
  5.4 1.3 %near.1 = (f32[5,4,56,128]{3,2,1,0:T(8,128)S(1)}, f32[8,3,4,56,128]{4,3,2,1,0:T(8,128)S(1)}) custom-call(f32[48,512]{1,0:T(8,128)S(1)} %collective-permute-done.1.refs_0_, f32[12,8,512]{2,1,0:T(8,128)S(1)} %get-tuple-element.18.refs_1_, bf16[512,512]{1,0:T(8,128)(2,1)S(1)} %get-tuple-element.19.refs_2_, ...), custom_call_target="tpu_custom_call", output_to_operand_aliasing={{0}: (4, {}), {1}: (5, {})} | custom-call | flops 1000000000 | bytes 10000000 | tf_op jit(solution)/shard_map/near/pallas_call | solution.py:495
  6.7 0.0 collective-permute-done.refs_0_
  6.7 3.8 %parareal.1 = (f32[1,3,32,512]{3,2,1,0:T(8,128)}, f32[5,4,56,128]{3,2,1,0:T(8,128)S(1)}, f32[8,3,4,56,128]{4,3,2,1,0:T(8,128)S(1)}) custom-call(f32[48,512]{1,0:T(8,128)S(1)} %collective-permute-done.refs_0_, f32[12,8,512]{2,1,0:T(8,128)S(1)} %get-tuple-element.18.refs_1_, ...), custom_call_target="tpu_custom_call", output_to_operand_aliasing={{1}: (6, {}), {2}: (7, {})} | custom-call | tf_op jit(solution)/shard_map/parareal/pallas_call | solution.py:506
  (1 shorter events, 0.0 us)
Async XLA Ops:
  1.1 4.3 %collective-permute-start.1 = (f32[48,512]{1,0:T(8,128)S(1)}, f32[48,512]{1,0:T(8,128)S(1)}, u32[]{:S(2)}, u32[]{:S(2)}) collective-permute-start(f32[48,512]{1,0:T(8,128)S(1)} %get-tuple-element.23), channel_id=1, source_target_pairs={{0,1},{1,0},{2,3},{3,2},{4,5},{5,4},{6,7},{7,6},{8,9},{9,8},{10,11... | collective-permute-start | bytes 294920 | tf_op jit(solution)/shard_map/ppermute | solution.py:463
  1.8 4.9 %collective-permute-start = (f32[48,512]{1,0:T(8,128)S(1)}, f32[48,512]{1,0:T(8,128)S(1)}, u32[]{:S(2)}, u32[]{:S(2)}) collective-permute-start(f32[48,512]{1,0:T(8,128)S(1)} %get-tuple-element.17), channel_id=1, source_target_pairs={{0,3},{1,2},{2,1},{3,0},{4,7},{5,6},{6,5},{7,4},{8,11},{9,10},{10,... | collective-permute-start | bytes 294920 | tf_op jit(solution)/shard_map/ppermute | solution.py:462

commit v3 on v2

--- a/solution.py
+++ b/solution.py
@@ -69,12 +69,14 @@
         start = pl.multiple_of(index * DEAL_ROWS, DEAL_ROWS)
         row = start + lax.broadcasted_iota(jnp.int32, (DEAL_ROWS, LANES), 0)
         lane = lax.broadcasted_iota(jnp.int32, (DEAL_ROWS, LANES), 1)
-        place = row % LANES * tiles + row // LANES
+        there = row - lane * tiles
+        tile = start // LANES
+        back = (row - tile * LANES) * tiles + tile - lane
         for t in range(tiles):
-            hit = row == lane * tiles + t
-            dealing[pl.ds(start, DEAL_ROWS), lanes(t)] = jnp.where(hit, 1.0, 0.0).astype(jnp.bfloat16)
-            hit = place == lane + t * LANES
-            undealing[pl.ds(start, DEAL_ROWS), lanes(t)] = jnp.where(hit, 1.0, 0.0).astype(jnp.bfloat16)
+            hit = jnp.where(there == t, 1.0, 0.0)
+            dealing[pl.ds(start, DEAL_ROWS), lanes(t)] = hit.astype(jnp.bfloat16)
+            hit = jnp.where(back == t * LANES, 1.0, 0.0)
+            undealing[pl.ds(start, DEAL_ROWS), lanes(t)] = hit.astype(jnp.bfloat16)
         return carry
 
     lax.fori_loop(0, tiles * LANES // DEAL_ROWS, block, 0)

time: 10.7 us -> 10.7 us (level)
  no operation moved by 1% of the time
where the time goes in v3:
time: 10.7 us; the launch traced here: 10.6 us
  Pallas kernels  7.58 us (71%)
  starting transfers between devices  1.94 us (18%)
  other arithmetic  1 us (9%)
    pallas_call x1, Pallas kernels, body(): pl.pallas_call(lambda *refs: kernel(cells, tiles, *refs), out_shape=(shap...  3.84 us
    pallas_call x1, Pallas kernels, body(): pl.pallas_call(lambda *refs: prepare(cells, tiles, *refs), out_shape=(fie...  2.36 us
    pallas_call x1, Pallas kernels, body(): pl.pallas_call(lambda *refs: near_side(cells, tiles, *refs), out_shape=(s...  1.33 us
    ppermute x1, starting transfers between devices, body(): lax.ppermute(outer, 'lon', [(k, (k + 1 if k % 2 else k - 1) % count) for...  1.2 us
    concatenate x1, other arithmetic, body(): jnp.concatenate([start.reshape(-1, lat_cells), depth, table], axis=0)  1 us
    ppermute x1, starting transfers between devices, body(): inner = lax.ppermute(inner, 'lon', [(k, k ^ 1) for k in ring])  0.74 us
  transfers between devices with their start and end apart: 2, of which 0 were waited for; matrix products, arithmetic and copies ran while one was open for 0% of the time, Pallas kernels for 35%

profile of v3, /device:TPU:27, one launch (start us, length us, event | category | flops | bytes accessed | tf_op | source)
XLA Modules:
  0.0 10.6 jit_solution(5457552562883527101)
XLA Ops:
  0.0 1.0 %pad_maximum_fusion.refs_0_ = f32[140,512]{1,0:T(8,128)S(1)} fusion(f32[12,512]{1,0:T(8,128)} %constant.2.clone, f32[32,512]{1,0:T(8,128)} %param.4, f32[96,512]{1,0:T(8,128)} %bitcast.1), kind=kLoop, calls=%fused_computation | loop fusion | flops 143360 | bytes 573440 | tf_op jit(solution)/shard_map/concatenate | solution.py:452
  1.1 0.7 %collective-permute-start.1 = (f32[48,512]{1,0:T(8,128)S(1)}, f32[48,512]{1,0:T(8,128)S(1)}, u32[]{:S(2)}, u32[]{:S(2)}) collective-permute-start(f32[48,512]{1,0:T(8,128)S(1)} %get-tuple-element.23), channel_id=1, source_target_pairs={{0,1},{1,0},{2,3},{3,2},{4,5},{5,4},{6,7},{7,6},{8,9},{9,8},{10,11... | collective-permute-start | bytes 294920 | tf_op jit(solution)/shard_map/ppermute | solution.py:465
  1.8 1.2 %collective-permute-start = (f32[48,512]{1,0:T(8,128)S(1)}, f32[48,512]{1,0:T(8,128)S(1)}, u32[]{:S(2)}, u32[]{:S(2)}) collective-permute-start(f32[48,512]{1,0:T(8,128)S(1)} %get-tuple-element.17), channel_id=1, source_target_pairs={{0,3},{1,2},{2,1},{3,0},{4,7},{5,6},{6,5},{7,4},{8,11},{9,10},{10,... | collective-permute-start | bytes 294920 | tf_op jit(solution)/shard_map/ppermute | solution.py:464
  3.0 2.4 %prepare.1 = (f32[5,4,56,128]{3,2,1,0:T(8,128)S(1)}, f32[2,4,32,128]{3,2,1,0:T(8,128)S(1)}, f32[12,8,512]{2,1,0:T(8,128)S(1)}, bf16[512,512]{1,0:T(8,128)(2,1)S(...) custom-call(f32[140,512]{1,0:T(8,128)S(1)} %pad_maximum_fusion.refs_0_), custom_call_target="tpu_custom_call" | custom-call | flops 1000000000 | bytes 10000000 | tf_op jit(solution)/shard_map/prepare/pallas_call | solution.py:479
  5.4 0.0 collective-permute-done.1.refs_0_
  5.4 1.3 %near.1 = (f32[5,4,56,128]{3,2,1,0:T(8,128)S(1)}, f32[8,3,4,56,128]{4,3,2,1,0:T(8,128)S(1)}) custom-call(f32[48,512]{1,0:T(8,128)S(1)} %collective-permute-done.1.refs_0_, f32[12,8,512]{2,1,0:T(8,128)S(1)} %get-tuple-element.18.refs_1_, bf16[512,512]{1,0:T(8,128)(2,1)S(1)} %get-tuple-element.19.refs_2_, ...), custom_call_target="tpu_custom_call", output_to_operand_aliasing={{0}: (4, {}), {1}: (5, {})} | custom-call | flops 1000000000 | bytes 10000000 | tf_op jit(solution)/shard_map/near/pallas_call | solution.py:497
  6.7 0.0 collective-permute-done.refs_0_
  6.7 3.8 %parareal.1 = (f32[1,3,32,512]{3,2,1,0:T(8,128)}, f32[5,4,56,128]{3,2,1,0:T(8,128)S(1)}, f32[8,3,4,56,128]{4,3,2,1,0:T(8,128)S(1)}) custom-call(f32[48,512]{1,0:T(8,128)S(1)} %collective-permute-done.refs_0_, f32[12,8,512]{2,1,0:T(8,128)S(1)} %get-tuple-element.18.refs_1_, ...), custom_call_target="tpu_custom_call", output_to_operand_aliasing={{1}: (6, {}), {2}: (7, {})} | custom-call | tf_op jit(solution)/shard_map/parareal/pallas_call | solution.py:508
  (1 shorter events, 0.0 us)
Async XLA Ops:
  1.1 4.3 %collective-permute-start.1 = (f32[48,512]{1,0:T(8,128)S(1)}, f32[48,512]{1,0:T(8,128)S(1)}, u32[]{:S(2)}, u32[]{:S(2)}) collective-permute-start(f32[48,512]{1,0:T(8,128)S(1)} %get-tuple-element.23), channel_id=1, source_target_pairs={{0,1},{1,0},{2,3},{3,2},{4,5},{5,4},{6,7},{7,6},{8,9},{9,8},{10,11... | collective-permute-start | bytes 294920 | tf_op jit(solution)/shard_map/ppermute | solution.py:465
  1.8 4.9 %collective-permute-start = (f32[48,512]{1,0:T(8,128)S(1)}, f32[48,512]{1,0:T(8,128)S(1)}, u32[]{:S(2)}, u32[]{:S(2)}) collective-permute-start(f32[48,512]{1,0:T(8,128)S(1)} %get-tuple-element.17), channel_id=1, source_target_pairs={{0,3},{1,2},{2,1},{3,0},{4,7},{5,6},{6,5},{7,4},{8,11},{9,10},{10,... | collective-permute-start | bytes 294920 | tf_op jit(solution)/shard_map/ppermute | solution.py:464
